TPU v7x, 32 devices: a whole 2x2x4 slice. The times are simulated.
32 devices in a mesh: groups: 2 (over y), row: 4 (over z), col: 2 (over x), sub: 2 (over core).
Axes of the slice: x: 2, y: 2, z: 4, core: 2. Of those that a mesh axis runs over, the one named last changes fastest.
Arguments:
- stream_in: bfloat16 [4096, 5376], P(('groups', 'row'), ('col', 'sub')), parts along dimension 0, may hold values from -6 to 6
- in_gain: float32 [5376], replicated, may hold values from 0.1 to 1.9
- query_weight: bfloat16 [5376, 4096], P('row', ('col', 'sub')), may hold values from -0.078125 to 0.078125
- key_matrix: bfloat16 [5376, 2048], P('row', ('col', 'sub')), may hold values from -0.078125 to 0.078125
- value_matrix: bfloat16 [5376, 2048], P('row', ('col', 'sub')), may hold values from -0.078125 to 0.078125
- query_gain: float32 [128], replicated, may hold values from 0.45 to 10, as said below
- key_norm_gain: float32 [128], replicated, may hold values from 0.45 to 10, as said below
- output_weight: bfloat16 [4096, 5376], P('row', ('col', 'sub')), may hold values from -3 to 3
- post_gain: float32 [5376], P(('col', 'sub')), may hold values from 0.1 to 1.9
Outputs:
- stream_out: bfloat16 [4096, 5376], P(('groups', 'row'), ('col', 'sub')), parts along dimension 0
There are 2 independent parts, one for each index of `groups`. A program takes and returns all parts, laid end to end along the dimension named above; an argument that names none is the same for every part. Nothing has to cross between parts.
Inputs may be any that keep to these rules, and one draw needn't show every extreme that they name: `query_gain`: positive. `key_norm_gain`: positive.
All inputs are finite; a program needn't handle non-finite values.
Results may differ from a plain program's by a relative error of at most 0.014.
The roundings to bfloat16 on the way count: a program that leaves them out, or rounds other values in their place, can miss the bound.
Values may be sent and summed in bfloat16 or wider, within the bound.
A program may use at most 128 MiB of HBM per device.

v0:
```python
import jax
import jax.numpy as jnp
from jax import lax
from jax.sharding import PartitionSpec as P

MODEL_WIDTH = 5376
QUERY_HEAD_COUNT = 32
WINDOW_LENGTH = 1024
EPSILON = 1e-06


def shifted(x, axis, by):
    count = lax.axis_size(axis)
    pairs = [(i, i + by) for i in range(count) if 0 <= i + by < count]
    return lax.ppermute(x, axis, pairs)


def root_mean_scale(values, gain):
    return values * lax.rsqrt(jnp.mean(values * values, axis=-1, keepdims=True) + EPSILON) * gain


def apply_rotary(tensor, token_positions):
    half_dim = tensor.shape[-1] // 2
    inverse = 10000.0 ** (-(jnp.arange(half_dim, dtype=jnp.float32) * 2.0) / tensor.shape[-1])
    angles = token_positions[:, None] * inverse[None, :]
    cosine = jnp.cos(angles)[:, None, :]
    sine_part = jnp.sin(angles)[:, None, :]
    first_half = tensor[..., :half_dim]
    second_half = tensor[..., half_dim:]
    return jnp.concatenate(
        [
            first_half * cosine - second_half * sine_part,
            second_half * cosine + first_half * sine_part,
        ],
        axis=-1,
    )


def on_device(
    stream_in,
    in_gain,
    query_weight,
    key_matrix,
    value_matrix,
    query_gain,
    key_norm_gain,
    output_weight,
    post_gain,
):
    token_rows = lax.all_gather(stream_in, ("col", "sub"), axis=1, tiled=True)
    tokens = token_rows.shape[0]
    normed = root_mean_scale(token_rows.astype(jnp.float32), in_gain).astype(jnp.bfloat16)

    def add_panel(panel_piece):
        return jnp.dot(normed, panel_piece, preferred_element_type=jnp.float32)

    query_proj = add_panel(lax.all_gather(query_weight, "row", axis=0, tiled=True))
    projected_keys = add_panel(lax.all_gather(key_matrix, "row", axis=0, tiled=True))
    projected_values = add_panel(lax.all_gather(value_matrix, "row", axis=0, tiled=True))
    head_size = query_gain.shape[0]
    query_heads = query_weight.shape[1] // head_size
    pair_heads = key_matrix.shape[1] // head_size
    group_count = query_heads // pair_heads
    scale_factor = float(MODEL_WIDTH // QUERY_HEAD_COUNT) ** (-0.5)
    row_index = lax.axis_index("row")
    query_places = row_index * tokens + jnp.arange(tokens, dtype=jnp.int32)
    query_rot = apply_rotary(
        root_mean_scale(query_proj.reshape(tokens, query_heads, head_size), query_gain),
        query_places.astype(jnp.float32),
    ).astype(jnp.bfloat16)
    rotary_keys = apply_rotary(
        root_mean_scale(projected_keys.reshape(tokens, pair_heads, head_size), key_norm_gain),
        query_places.astype(jnp.float32),
    ).astype(jnp.bfloat16)
    keys_flat = rotary_keys.reshape(tokens, pair_heads * head_size)
    values_flat = projected_values.astype(jnp.bfloat16)
    shards_back = min(WINDOW_LENGTH // tokens, lax.axis_size("row") - 1)
    band_length = (shards_back + 1) * tokens
    key_parts = [keys_flat]
    value_parts = [values_flat]
    for offset in range(1, shards_back + 1):
        keys_prior, values_prior = shifted((keys_flat, values_flat), "row", offset)
        key_parts = [keys_prior] + key_parts
        value_parts = [values_prior] + value_parts
    keys_band = jnp.concatenate(key_parts, axis=0)
    values_band = jnp.concatenate(value_parts, axis=0)
    key_places = (row_index - shards_back) * tokens + jnp.arange(band_length, dtype=jnp.int32)
    distance = query_places[:, None] - key_places[None, :]
    visible = (distance >= 0) & (distance < WINDOW_LENGTH) & (key_places[None, :] >= 0)
    grouped = query_rot.reshape(tokens, pair_heads, group_count, head_size)
    scores = (
        jnp.einsum(
            "qhgd,shd->hgqs",
            grouped,
            keys_band.reshape(band_length, pair_heads, head_size),
            preferred_element_type=jnp.float32,
        )
        * scale_factor
    )
    scores = jnp.where(visible, scores, -1e30)
    row_max = jnp.max(scores, axis=-1, keepdims=True)
    exponent = jnp.exp(scores - row_max)
    weights = (exponent / jnp.sum(exponent, axis=-1, keepdims=True)).astype(jnp.bfloat16)
    attended = jnp.einsum(
        "hgqs,shd->qhgd",
        weights,
        values_band.reshape(band_length, pair_heads, head_size),
        preferred_element_type=jnp.float32,
    )
    heads_out = attended.reshape(tokens, query_heads * head_size).astype(jnp.bfloat16)
    head_rows = lax.all_gather(heads_out, ("col", "sub"), axis=1, tiled=True)
    branch = jnp.dot(
        head_rows,
        lax.all_gather(output_weight, "row", axis=0, tiled=True),
        preferred_element_type=jnp.float32,
    )
    squares = lax.psum(jnp.sum(branch * branch, axis=-1), ("col", "sub"))
    scaled = branch * lax.rsqrt(squares[:, None] / MODEL_WIDTH + EPSILON) * post_gain
    return (stream_in.astype(jnp.float32) + scaled).astype(jnp.bfloat16)


def swapped(x):
    count = lax.axis_size("groups")
    return lax.ppermute(x, "groups", [(i, count - 1 - i) for i in range(count)])


def rows_gathered(piece):
    return lax.all_gather(piece, "row", axis=0)


def attend(query_rot, keys_flat, values_flat, row_index, head_size, scale_factor):
    tokens, kv_width = keys_flat.shape
    pair_heads = kv_width // head_size
    group_count = query_rot.shape[1] // pair_heads
    query_places = row_index * tokens + jnp.arange(tokens, dtype=jnp.int32)
    shards_back = min(WINDOW_LENGTH // tokens, lax.axis_size("row") - 1)
    band_length = (shards_back + 1) * tokens
    key_parts = [keys_flat]
    value_parts = [values_flat]
    for offset in range(1, shards_back + 1):
        keys_prior, values_prior = shifted((keys_flat, values_flat), "row", offset)
        key_parts = [keys_prior] + key_parts
        value_parts = [values_prior] + value_parts
    keys_band = jnp.concatenate(key_parts, axis=0)
    values_band = jnp.concatenate(value_parts, axis=0)
    key_places = (row_index - shards_back) * tokens + jnp.arange(band_length, dtype=jnp.int32)
    distance = query_places[:, None] - key_places[None, :]
    visible = (distance >= 0) & (distance < WINDOW_LENGTH) & (key_places[None, :] >= 0)
    grouped = query_rot.reshape(tokens, pair_heads, group_count, head_size)
    scores = (
        jnp.einsum(
            "qhgd,shd->hgqs",
            grouped,
            keys_band.reshape(band_length, pair_heads, head_size),
            preferred_element_type=jnp.float32,
        )
        * scale_factor
    )
    scores = jnp.where(visible, scores, -1e30)
    row_max = jnp.max(scores, axis=-1, keepdims=True)
    exponent = jnp.exp(scores - row_max)
    weights = (exponent / jnp.sum(exponent, axis=-1, keepdims=True)).astype(jnp.bfloat16)
    attended = jnp.einsum(
        "hgqs,shd->qhgd",
        weights,
        values_band.reshape(band_length, pair_heads, head_size),
        preferred_element_type=jnp.float32,
    )
    return attended.reshape(tokens, -1).astype(jnp.bfloat16)


def on_device_sharing(
    stream_in,
    in_gain,
    query_weight,
    key_matrix,
    value_matrix,
    query_gain,
    key_norm_gain,
    output_weight,
    post_gain,
):
    group = lax.axis_index("groups")
    head_size = query_gain.shape[0]
    rows = lax.axis_size("row")

    def own_columns(w):
        width = w.shape[1] // 2
        return lax.dynamic_slice_in_dim(w, group * width, width, axis=1)

    def halves(w):
        own = rows_gathered(own_columns(w))
        other = swapped(own)
        full = rows * w.shape[0]
        return (own.reshape(full, -1), other.reshape(full, -1))

    key_halves = halves(key_matrix)
    token_rows = lax.all_gather(stream_in, ("col", "sub"), axis=1, tiled=True)
    value_halves = halves(value_matrix)
    query_halves = halves(query_weight)
    depth = output_weight.shape[0]
    half, quarter = (depth // 2, depth // 4)
    out_own = rows_gathered(lax.dynamic_slice_in_dim(output_weight, group * half, half, axis=0))
    out_peer = swapped(out_own[:, :quarter])
    out_direct = rows_gathered(
        lax.dynamic_slice_in_dim(output_weight, (1 - group) * half + quarter, quarter, axis=0)
    )
    tokens = token_rows.shape[0]
    normed = root_mean_scale(token_rows.astype(jnp.float32), in_gain).astype(jnp.bfloat16)

    def add_panel(panel):
        return jnp.dot(normed, panel, preferred_element_type=jnp.float32)

    scale_factor = float(MODEL_WIDTH // QUERY_HEAD_COUNT) ** (-0.5)
    row_index = lax.axis_index("row")
    places = (row_index * tokens + jnp.arange(tokens, dtype=jnp.int32)).astype(jnp.float32)

    def rotated(projected, gain):
        heads = projected.reshape(tokens, -1, head_size)
        return apply_rotary(root_mean_scale(heads, gain), places).astype(jnp.bfloat16)

    attended = []
    for i in range(2):
        keys_flat = rotated(add_panel(key_halves[i]), key_norm_gain).reshape(tokens, -1)
        values_flat = add_panel(value_halves[i]).astype(jnp.bfloat16)
        query_rot = rotated(add_panel(query_halves[i]), query_gain)
        heads_out = attend(query_rot, keys_flat, values_flat, row_index, head_size, scale_factor)
        attended.append(lax.all_gather(heads_out, ("col", "sub"), axis=1, tiled=True))
    own_rows, other_rows = attended
    blocks = other_rows.reshape(tokens, -1, half)
    branch = (
        jnp.dot(
            own_rows, out_own.reshape(-1, out_own.shape[-1]), preferred_element_type=jnp.float32
        )
        + jnp.dot(
            blocks[:, :, quarter:].reshape(tokens, -1),
            out_direct.reshape(-1, out_direct.shape[-1]),
            preferred_element_type=jnp.float32,
        )
        + jnp.dot(
            blocks[:, :, :quarter].reshape(tokens, -1),
            out_peer.reshape(-1, out_peer.shape[-1]),
            preferred_element_type=jnp.float32,
        )
    )
    squares = lax.psum(jnp.sum(branch * branch, axis=-1), ("col", "sub"))
    scaled = branch * lax.rsqrt(squares[:, None] / MODEL_WIDTH + EPSILON) * post_gain
    return (stream_in.astype(jnp.float32) + scaled).astype(jnp.bfloat16)


def on_device_any(*operands):
    head_size = operands[5].shape[0]
    pair_heads = operands[3].shape[1] // head_size
    blocks_agree = lax.axis_size("row") == lax.axis_size("col") * lax.axis_size("sub")
    if lax.axis_size("groups") == 2 and pair_heads % 2 == 0 and blocks_agree:
        return on_device_sharing(*operands)
    return on_device(*operands)


def solution(mesh):
    placed = (
        P(("groups", "row"), ("col", "sub")),
        P(),
        P("row", ("col", "sub")),
        P("row", ("col", "sub")),
        P("row", ("col", "sub")),
        P(),
        P(),
        P("row", ("col", "sub")),
        P(("col", "sub")),
    )
    return jax.shard_map(
        on_device_any,
        mesh=mesh,
        in_specs=placed,
        out_specs=P(("groups", "row"), ("col", "sub")),
        check_vma=False,
    )
```

profile of v0, /device:TPU:22, one launch (start us, length us, event | category | flops | bytes accessed | tf_op | source)
XLA Modules:
  0.0 608.8 jit_solution(1578314653373979051)
XLA Ops:
  15.3 50.3 %all-gather.22.cloned.1.call-done = bf16[5376,256]{1,0:T(8,128)(2,1)} async-done(((bf16[1344,256]{1,0:T(8,128)(2,1)}), bf16[5376,256]{1,0:T(8,128)(2,1)}) %all-gather.22.cloned.1.call-update) | async-done | bytes 2752528 | tf_op jit(solution)/shard_map/all_gather | solution.py:128
  67.8 100.0 %all-gather.24.cloned.1.call-done = bf16[5376,512]{1,0:T(8,128)(2,1)} async-done(((bf16[1344,512]{1,0:T(8,128)(2,1)}), bf16[5376,512]{1,0:T(8,128)(2,1)}) %all-gather.24.cloned.1.call-update) | async-done | bytes 5505040 | tf_op jit(solution)/shard_map/all_gather | solution.py:128
  173.6 51.5 %all-gather.20.cloned.1.call-done = bf16[5376,256]{1,0:T(8,128)(2,1)} async-done(((bf16[1344,256]{1,0:T(8,128)(2,1)}), bf16[5376,256]{1,0:T(8,128)(2,1)}) %all-gather.20.cloned.1.call-update) | async-done | bytes 2752528 | tf_op jit(solution)/shard_map/all_gather | solution.py:128
  230.3 37.3 %all-gather.14.cloned.1.call-done = bf16[512,5376]{0,1:T(8,128)(2,1)} async-done(((bf16[512,1344]{0,1:T(8,128)(2,1)}), bf16[512,5376]{0,1:T(8,128)(2,1)}) %all-gather.14.cloned.1.call-update) | async-done | bytes 5505040 | tf_op jit(solution)/shard_map/all_gather | solution.py:198
  283.8 63.6 %collective-permute-done.4 = bf16[4,1344,256]{2,1,0:T(8,128)(2,1)} collective-permute-done((bf16[4,1344,256]{2,1,0:T(8,128)(2,1)}, bf16[4,1344,256]{2,1,0:T(8,128)(2,1)}, u32[]{:S(2)}, u32[]{:S(2)}) %collective-permute-start.4) | collective-permute-done | bytes 2752544 | tf_op jit(solution)/shard_map/ppermute | solution.py:124
  356.3 8.2 %copy.30 = bf16[512,5376]{1,0:T(8,128)(2,1)} copy(bf16[512,5376]{0,1:T(8,128)(2,1)} %bitcast.135) | data formatting | bytes 11010048 | tf_op jit(solution)/shard_map/dot_general | solution.py:212
  364.6 8.3 %multiply_reduce_fusion.2 = (f32[512,4]{0,1:T(4,128)S(1)}, f32[512,4,128]{0,2,1:T(8,128)}) fusion(bf16[4,128,5376]{2,1,0:T(8,128)(2,1)} %bitcast.137, f32[5376]{0:T(1024)S(1)} %copy-done.11, f32[512]{0:T(512)S(1)} %add_rsqrt_fusion.5, bf16[512,5376]{0,1:T(8,128)(2,1)} %all-gather.14.cloned.1.call-done), kind=kOutput, calls=%fused_computation.52 | convolution fusion | flops 2830104576 | bytes 12090368 | tf_op jit(solution)/shard_map/dot_general | solution.py:212
  372.9 23.0 %collective-permute-done.6 = bf16[512,256]{1,0:T(8,128)(2,1)S(1)} collective-permute-done((bf16[512,256]{1,0:T(8,128)(2,1)S(1)}, bf16[512,256]{1,0:T(8,128)(2,1)S(1)}, u32[]{:S(2)}, u32[]{:S(2)}) %collective-permute-start.6) | collective-permute-done | bytes 262176 | tf_op jit(solution)/shard_map/ppermute | solution.py:15
  397.1 8.1 %copy.39 = bf16[512,5376]{1,0:T(8,128)(2,1)} copy(bf16[512,5376]{0,1:T(8,128)(2,1)} %bitcast.35) | data formatting | bytes 11010048 | tf_op jit(solution)/shard_map/dot_general | solution.py:212
  405.1 7.4 %multiply_reduce_fusion.1 = (f32[512,4]{0,1:T(4,128)S(1)}, f32[512,4,128]{0,2,1:T(8,128)S(1)}) fusion(bf16[4,128,5376]{2,1,0:T(8,128)(2,1)} %bitcast.136, f32[5376]{0:T(1024)S(1)} %copy-done.11, f32[512]{0:T(512)S(1)} %add_rsqrt_fusion.5, bf16[512,5376]{0,1:T(8,128)(2,1)} %all-gather.14.cloned.1.call-done), kind=kOutput, calls=%fused_computation.50 | convolution fusion | flops 2830104576 | bytes 12090368 | tf_op jit(solution)/shard_map/dot_general | solution.py:212
  414.0 11.0 %fusion.55 = (f32[2,2,512]{2,1,0:T(2,128)S(1)}, f32[2,2,512,1536]{2,3,1,0:T(8,128)}) fusion(pred[512,1536]{0,1:T(8,128)(4,1)} %fusion.25, bf16[512,2,128]{0,2,1:T(8,128)(2,1)} %maximum_convert_fusion.1, bf16[512,2,128]{0,2,1:T(8,128)(2,1)} %bitcast.30, bf16[512,2,128]{0,2,1:T(8,128)(2,1)} %bitcast.29, bf16[512,2,2,64]{3,0,2,1:T(8,128)(2,1)S(1)} %copy.42, ...), kind=kOutput, calls=%fused_computation.101 | convolution fusion | flops 821298688 | bytes 14688256 | tf_op jit(solution)/shard_map/sub | solution.py:161
  425.0 6.4 %fusion.30 = bf16[2,128,2,512]{3,1,2,0:T(8,128)(2,1)} fusion(bf16[1536,2,128,1]{0,2,3,1:T(8,128)(2,1)S(1)} %bitcast.147, f32[2,2,512,1536]{2,3,1,0:T(8,128)} %get-tuple-element.32, f32[2,2,512]{2,1,0:T(2,128)S(1)} %get-tuple-element.31), kind=kOutput, calls=%fused_computation.43 | convolution fusion | flops 811859968 | bytes 13901824 | tf_op jit(solution)/shard_map/hgqs,shd->qhgd/dot_general | solution.py:163
  431.7 6.0 convolution_convert_fusion.1
  444.9 10.4 %collective-permute-done = bf16[512,256]{1,0:T(8,128)(2,1)S(1)} collective-permute-done((bf16[512,256]{1,0:T(8,128)(2,1)S(1)}, bf16[512,256]{1,0:T(8,128)(2,1)S(1)}, u32[]{:S(2)}, u32[]{:S(2)}) %collective-permute-start) | collective-permute-done | bytes 262176 | tf_op jit(solution)/shard_map/ppermute | solution.py:15
  455.3 25.9 %collective-permute-done.1 = bf16[512,256]{1,0:T(8,128)(2,1)S(1)} collective-permute-done((bf16[512,256]{1,0:T(8,128)(2,1)S(1)}, bf16[512,256]{1,0:T(8,128)(2,1)S(1)}, u32[]{:S(2)}, u32[]{:S(2)}) %collective-permute-start.1) | collective-permute-done | bytes 262176 | tf_op jit(solution)/shard_map/ppermute | solution.py:15
  482.2 10.9 %collective-permute-done.3 = bf16[512,256]{0,1:T(8,128)(2,1)} collective-permute-done((bf16[512,256]{0,1:T(8,128)(2,1)}, bf16[512,256]{0,1:T(8,128)(2,1)}, u32[]{:S(2)}, u32[]{:S(2)}) %collective-permute-start.3) | collective-permute-done | bytes 262176 | tf_op jit(solution)/shard_map/ppermute | solution.py:15
  493.0 10.7 %fusion.56 = (f32[2,2,512]{2,1,0:T(2,128)S(1)}, f32[2,2,512,1536]{2,3,1,0:T(8,128)}) fusion(pred[512,1536]{0,1:T(8,128)(4,1)S(1)} %copy-done.4, bf16[512,2,128]{0,2,1:T(8,128)(2,1)} %maximum_convert_fusion, bf16[512,2,128]{0,2,1:T(8,128)(2,1)} %bitcast.8, bf16[512,2,128]{0,2,1:T(8,128)(2,1)} %bitcast.7, bf16[512,2,2,64]{3,0,2,1:T(8,128)(2,1)S(1)} %copy.33, ...), kind=kOutput, calls=%fused_computation.102 | convolution fusion | flops 821298688 | bytes 14688256 | tf_op jit(solution)/shard_map/sub | solution.py:161
  503.7 6.4 %fusion.31 = bf16[2,128,2,512]{3,1,2,0:T(8,128)(2,1)} fusion(bf16[1536,2,128,1]{0,2,3,1:T(8,128)(2,1)S(1)} %bitcast.148, f32[2,2,512,1536]{2,3,1,0:T(8,128)} %get-tuple-element.34, f32[2,2,512]{2,1,0:T(2,128)S(1)} %get-tuple-element.33), kind=kOutput, calls=%fused_computation.44 | convolution fusion | flops 811859968 | bytes 13901824 | tf_op jit(solution)/shard_map/hgqs,shd->qhgd/dot_general | solution.py:163
  510.2 8.6 %copy.50 = bf16[2048,1344]{1,0:T(8,128)(2,1)} copy(bf16[2048,1344]{0,1:T(8,128)(2,1)} %all-gather.26.cloned.1.call-done) | data formatting | bytes 11010048 | tf_op jit(solution)/shard_map/all_gather | solution.py:128
  530.7 5.4 convolution_bitcast_fusion.1
  536.0 7.3 %convolution_add_fusion = f32[512,1344]{0,1:T(8,128)S(1)} fusion(f32[512,1344]{0,1:T(8,128)} %convolution_bitcast_fusion.1, bf16[2048,1344]{0,1:T(8,128)(2,1)} %all-gather.26.cloned.1.call-done, bf16[512,2048]{0,1:T(8,128)(2,1)} %all-gather.16.cloned.1.call-done), kind=kOutput, calls=%fused_computation.33 | convolution fusion | flops 2819260416 | bytes 13107200 | tf_op jit(solution)/shard_map/dot_general | solution.py:232
  543.3 43.6 %collective-permute-done.11 = bf16[4,256,1344]{1,2,0:T(8,128)(2,1)} collective-permute-done((bf16[4,256,1344]{1,2,0:T(8,128)(2,1)S(1)}, bf16[4,256,1344]{1,2,0:T(8,128)(2,1)}, u32[]{:S(2)}, u32[]{:S(2)}) %collective-permute-start.11) | collective-permute-done | bytes 2752544 | tf_op jit(solution)/shard_map/ppermute | solution.py:124
  586.9 5.1 multiply_reduce_fusion
  592.1 5.9 psum.7
  (104 shorter events, 73.5 us)
Async XLA Ops:
  6.5 59.1 %all-gather.22.cloned.1.call-start = ((), (), s32[]{:S(2)}) async-start(), calls=%async_computation.4 | async-start | bytes 3440640 | tf_op jit(solution)/shard_map/all_gather | solution.py:128
  8.7 159.1 %all-gather.24.cloned.1.call-start = ((), (), s32[]{:S(2)}) async-start(), calls=%async_computation.5 | async-start | bytes 6881280 | tf_op jit(solution)/shard_map/all_gather | solution.py:128
  11.3 213.8 %all-gather.20.cloned.1.call-start = ((), (), s32[]{:S(2)}) async-start(), calls=%async_computation.3 | async-start | bytes 3440640 | tf_op jit(solution)/shard_map/all_gather | solution.py:128
  13.4 254.2 %all-gather.14.cloned.1.call-start = ((), (), s32[]{:S(2)}) async-start(), calls=%async_computation | async-start | bytes 6881280 | tf_op jit(solution)/shard_map/all_gather | solution.py:198
  14.0 496.2 %all-gather.26.cloned.1.call-start = ((), (), s32[]{:S(2)}) async-start(), calls=%async_computation.6 | async-start | bytes 6881280 | tf_op jit(solution)/shard_map/all_gather | solution.py:128
  15.3 510.8 %all-gather.28.cloned.1.call-start = ((), (), s32[]{:S(2)}) async-start(), calls=%async_computation.7 | async-start | bytes 3440640 | tf_op jit(solution)/shard_map/all_gather | solution.py:128
  65.6 160.1 %collective-permute-start.7 = (bf16[4,1344,256]{2,1,0:T(8,128)(2,1)}, bf16[4,1344,256]{2,1,0:T(8,128)(2,1)}, u32[]{:S(2)}, u32[]{:S(2)}) collective-permute-start(bf16[4,1344,256]{2,1,0:T(8,128)(2,1)} %bitcast.139), channel_id=1, source_target_pairs={{0,16},{16,0},{1,17},{17,1},{2,18},{18,2},{3,19},{19,3},{4,20},{20... | collective-permute-start | bytes 8257544 | tf_op jit(solution)/shard_map/ppermute | solution.py:124
  67.2 463.5 %all-gather.18.cloned.1.call-start = ((), (), s32[]{:S(2)}) async-start(), calls=%async_computation.2 | async-start | bytes 2621440 | tf_op jit(solution)/shard_map/all_gather | solution.py:228
  167.9 229.2 %collective-permute-start.10 = (bf16[4,1344,512]{2,1,0:T(8,128)(2,1)}, bf16[4,1344,512]{2,1,0:T(8,128)(2,1)}, u32[]{:S(2)}, u32[]{:S(2)}) collective-permute-start(bf16[4,1344,512]{2,1,0:T(8,128)(2,1)} %bitcast.134), channel_id=1, source_target_pairs={{0,16},{16,0},{1,17},{17,1},{2,18},{18,2},{3,19},{19,3},{4,20},{20... | collective-permute-start | bytes 16515080 | tf_op jit(solution)/shard_map/ppermute | solution.py:124
  225.1 122.3 %collective-permute-start.4 = (bf16[4,1344,256]{2,1,0:T(8,128)(2,1)}, bf16[4,1344,256]{2,1,0:T(8,128)(2,1)}, u32[]{:S(2)}, u32[]{:S(2)}) collective-permute-start(bf16[4,1344,256]{2,1,0:T(8,128)(2,1)} %bitcast.151), channel_id=1, source_target_pairs={{0,16},{16,0},{1,17},{17,1},{2,18},{18,2},{3,19},{19,3},{4,20},{20... | collective-permute-start | bytes 8257544 | tf_op jit(solution)/shard_map/ppermute | solution.py:124
  225.7 45.8 %copy-start.11 = (f32[5376]{0:T(1024)S(1)}, f32[5376]{0:T(1024)}, u32[]{:S(2)}) copy-start(f32[5376]{0:T(1024)} %param.10) | copy-start | bytes 64516
  279.1 134.9 %collective-permute-start.8 = (bf16[512,256]{0,1:T(8,128)(2,1)}, bf16[512,256]{0,1:T(8,128)(2,1)}, u32[]{:S(2)}, u32[]{:S(2)}) collective-permute-start(bf16[512,256]{0,1:T(8,128)(2,1)} %bitcast.28), channel_id=1, source_target_pairs={{0,8},{4,12},{1,9},{5,13},{2,10},{6,14},{3,11},{7,15},{16,24},{20,... | collective-permute-start | bytes 786440 | tf_op jit(solution)/shard_map/ppermute | solution.py:15
  280.4 133.6 %collective-permute-start.9 = (bf16[512,256]{0,1:T(8,128)(2,1)}, bf16[512,256]{0,1:T(8,128)(2,1)}, u32[]{:S(2)}, u32[]{:S(2)}) collective-permute-start(bf16[512,256]{0,1:T(8,128)(2,1)} %bitcast.28), channel_id=1, source_target_pairs={{0,4},{4,8},{8,12},{1,5},{5,9},{9,13},{2,6},{6,10},{10,14},{3,7},{... | collective-permute-start | bytes 786440 | tf_op jit(solution)/shard_map/ppermute | solution.py:15
  351.9 21.0 %collective-permute-start.5 = (bf16[512,256]{1,0:T(8,128)(2,1)S(1)}, bf16[512,256]{1,0:T(8,128)(2,1)S(1)}, u32[]{:S(2)}, u32[]{:S(2)}) collective-permute-start(bf16[512,256]{1,0:T(8,128)(2,1)S(1)} %convolution_convert_fusion), channel_id=1, source_target_pairs={{0,8},{4,12},{1,9},{5,13},{2,10},{6,14},{3,11},{7,15},{16,24},{20,... | collective-permute-start | bytes 786440 | tf_op jit(solution)/shard_map/ppermute | solution.py:15
  353.2 42.6 %collective-permute-start.6 = (bf16[512,256]{1,0:T(8,128)(2,1)S(1)}, bf16[512,256]{1,0:T(8,128)(2,1)S(1)}, u32[]{:S(2)}, u32[]{:S(2)}) collective-permute-start(bf16[512,256]{1,0:T(8,128)(2,1)S(1)} %convolution_convert_fusion), channel_id=1, source_target_pairs={{0,4},{4,8},{8,12},{1,5},{5,9},{9,13},{2,6},{6,10},{10,14},{3,7},{... | collective-permute-start | bytes 786440 | tf_op jit(solution)/shard_map/ppermute | solution.py:15
  431.5 61.5 %copy-start.4 = (pred[512,1536]{0,1:T(8,128)(4,1)S(1)}, pred[512,1536]{0,1:T(8,128)(4,1)}, u32[]{:S(2)}) copy-start(pred[512,1536]{0,1:T(8,128)(4,1)} %fusion.25) | copy-start | bytes 2359300
  431.5 104.5 %all-gather.16.cloned.1.call-start = ((), (), s32[]{:S(2)}) async-start(), calls=%async_computation.1 | async-start | bytes 2621440 | tf_op jit(solution)/shard_map/all_gather | solution.py:228
  437.7 17.6 %collective-permute-start = (bf16[512,256]{1,0:T(8,128)(2,1)S(1)}, bf16[512,256]{1,0:T(8,128)(2,1)S(1)}, u32[]{:S(2)}, u32[]{:S(2)}) collective-permute-start(bf16[512,256]{1,0:T(8,128)(2,1)S(1)} %convolution_convert_fusion.1), channel_id=1, source_target_pairs={{0,8},{4,12},{1,9},{5,13},{2,10},{6,14},{3,11},{7,15},{16,24},{20,... | collective-permute-start | bytes 786440 | tf_op jit(solution)/shard_map/ppermute | solution.py:15
  439.0 42.2 %collective-permute-start.1 = (bf16[512,256]{1,0:T(8,128)(2,1)S(1)}, bf16[512,256]{1,0:T(8,128)(2,1)S(1)}, u32[]{:S(2)}, u32[]{:S(2)}) collective-permute-start(bf16[512,256]{1,0:T(8,128)(2,1)S(1)} %convolution_convert_fusion.1), channel_id=1, source_target_pairs={{0,4},{4,8},{8,12},{1,5},{5,9},{9,13},{2,6},{6,10},{10,14},{3,7},{... | collective-permute-start | bytes 786440 | tf_op jit(solution)/shard_map/ppermute | solution.py:15
  441.7 40.4 %collective-permute-start.2 = (bf16[512,256]{0,1:T(8,128)(2,1)}, bf16[512,256]{0,1:T(8,128)(2,1)}, u32[]{:S(2)}, u32[]{:S(2)}) collective-permute-start(bf16[512,256]{0,1:T(8,128)(2,1)} %bitcast.6), channel_id=1, source_target_pairs={{0,8},{4,12},{1,9},{5,13},{2,10},{6,14},{3,11},{7,15},{16,24},{20,... | collective-permute-start | bytes 786440 | tf_op jit(solution)/shard_map/ppermute | solution.py:15
  443.0 50.0 %collective-permute-start.3 = (bf16[512,256]{0,1:T(8,128)(2,1)}, bf16[512,256]{0,1:T(8,128)(2,1)}, u32[]{:S(2)}, u32[]{:S(2)}) collective-permute-start(bf16[512,256]{0,1:T(8,128)(2,1)} %bitcast.6), channel_id=1, source_target_pairs={{0,4},{4,8},{8,12},{1,5},{5,9},{9,13},{2,6},{6,10},{10,14},{3,7},{... | collective-permute-start | bytes 786440 | tf_op jit(solution)/shard_map/ppermute | solution.py:15
  525.5 61.4 %collective-permute-start.11 = (bf16[4,256,1344]{1,2,0:T(8,128)(2,1)S(1)}, bf16[4,256,1344]{1,2,0:T(8,128)(2,1)}, u32[]{:S(2)}, u32[]{:S(2)}) collective-permute-start(bf16[4,256,1344]{1,2,0:T(8,128)(2,1)S(1)} %copy.75), channel_id=1, source_target_pairs={{0,16},{16,0},{1,17},{17,1},{2,18},{18,2},{3,19},{19,3},{4,20},{20... | collective-permute-start | bytes 8257544 | tf_op jit(solution)/shard_map/ppermute | solution.py:124
  536.0 50.9 %copy-start.10 = (bf16[512,2048]{0,1:T(8,128)(2,1)S(1)}, bf16[512,2048]{0,1:T(8,128)(2,1)}, u32[]{:S(2)}) copy-start(bf16[512,2048]{0,1:T(8,128)(2,1)} %all-gather.18.cloned.1.call-done) | copy-start | bytes 6291460
  543.3 54.6 %copy-start.7 = (f32[1344]{0:T(1024)S(1)}, f32[1344]{0:T(1024)}, u32[]{:S(2)}) copy-start(f32[1344]{0:T(1024)} %param.17) | copy-start | bytes 16132
  (9 other events, 70.4 us)
Sparse Core Ops, SparseCore 0:
  8.9 56.6 all-gather.21
  67.2 100.6 all-gather.23
  169.4 55.6 all-gather.19
  226.5 40.9 all-gather.13
  269.0 119.5 all-gather.25
  390.0 82.8 all-gather.27
  474.4 33.1 all-gather.17
  510.3 21.6 all-gather.15
where the time goes:
time: 618 us; the launch traced here: 609 us
  waiting for transfers between devices  417 us (67%)
  matrix products  84.1 us (14%)
  local copies, waits for them, and re-layouts  55.8 us (9%)
  starting transfers between devices  18.2 us (3%)
  between operations  14.1 us (2%)
  other arithmetic  13.6 us (2%)
    all_gather x5, waiting for transfers between devices, rows_gathered(): return lax.all_gather(piece, 'row', axis=0)  202 us
    ppermute x4, waiting for transfers between devices, swapped(): return lax.ppermute(x, 'groups', [(i, count - 1 - i) for i in range(count)])  107 us
    ppermute x8, waiting for transfers between devices, shifted(): return lax.ppermute(x, axis, pairs)  70.2 us
    all_gather x1, waiting for transfers between devices, on_device_sharing(): token_rows = lax.all_gather(stream_in, ('col', 'sub'), axis=1, tiled=True)  37.3 us
    dot_general x6, matrix products, add_panel(): return jnp.dot(normed, panel, preferred_element_type=jnp.float32)  31.8 us
    dot_general x4, local copies, waits for them, and re-layouts, add_panel(): return jnp.dot(normed, panel, preferred_element_type=jnp.float32)  24.2 us
    sub x2, matrix products, attend(): exponent = jnp.exp(scores - row_max)  21.7 us
    ppermute x8, starting transfers between devices, shifted(): return lax.ppermute(x, axis, pairs)  15.5 us
  transfers between devices with their start and end apart: 20, of which 10 were waited for; matrix products, arithmetic and copies ran while one was open for 23% of the time, Pallas kernels for 0%

commit v1 on v0

--- a/solution.py
+++ b/solution.py
@@ -195,7 +195,18 @@
         return (own.reshape(full, -1), other.reshape(full, -1))
 
     key_halves = halves(key_matrix)
-    token_rows = lax.all_gather(stream_in, ("col", "sub"), axis=1, tiled=True)
+    ways = lax.axis_size(("col", "sub"))
+    up = [(d, (d + 1) % ways) for d in range(ways)]
+    down = [(d, (d - 1) % ways) for d in range(ways)]
+    earlier, later = ([stream_in], [stream_in])
+    for _ in range(ways // 2):
+        earlier.append(lax.ppermute(earlier[-1], ("col", "sub"), up))
+    for _ in range((ways - 1) // 2):
+        later.append(lax.ppermute(later[-1], ("col", "sub"), down))
+    line = jnp.concatenate([*earlier[::-1], *later[1:]], axis=1)
+    token_rows = jnp.roll(
+        line, (lax.axis_index(("col", "sub")) - ways // 2) * stream_in.shape[1], axis=1
+    )
     value_halves = halves(value_matrix)
     query_halves = halves(query_weight)
     depth = output_weight.shape[0]

time: 618 us -> 576 us (0.932)
  waiting for transfers between devices: 417 us -> 347 us
  local copies, waits for them, and re-layouts: 55.8 us -> 72.3 us
  matrix products: 84.1 us -> 92.5 us
    all_gather x5, waiting for transfers between devices: 202 us -> 148 us  [rows_gathered(): return lax.all_gather(piece, 'row', axis=0)]
    ppermute x0 -> x3, waiting for transfers between devices: none -> 44.5 us  [the longest x2 44.5 us: on_device_sharing(): earlier.append(lax.ppermute(earlier[-1], ('col', 'sub'), up))]
    ppermute x4, waiting for transfers between devices: 107 us -> 67.6 us  [swapped(): return lax.ppermute(x, 'groups', [(i, count - 1 - i) for i in range(count)])]
    all_gather x1 -> x0, waiting for transfers between devices: 37.3 us -> none  [on_device_sharing(): token_rows = lax.all_gather(stream_in, ('col', 'sub'), axis=1, tiled=True)]
    ppermute x8, waiting for transfers between devices: 70.2 us -> 86.4 us  [shifted(): return lax.ppermute(x, axis, pairs)]
    unnamed x27 -> x38, local copies, waits for them, and re-layouts: 3.39 us -> 18.1 us
    dot_general x6, matrix products: 31.8 us -> 40.2 us  [add_panel(): return jnp.dot(normed, panel, preferred_element_type=jnp.float32)]
  transfers between devices with their start and end apart: 20 -> 22, of which waited for: 10 -> 11; matrix products, arithmetic and copies ran while one was open for 23% -> 30% of each run, Pallas kernels for 0% -> 0%
where the time goes in v1:
time: 576 us; the launch traced here: 566 us
  waiting for transfers between devices  347 us (60%)
  matrix products  92.5 us (16%)
  local copies, waits for them, and re-layouts  72.3 us (13%)
  starting transfers between devices  18.9 us (3%)
  other arithmetic  15.7 us (3%)
  between operations  14.4 us (2%)
  blocking collectives  5.97 us (1%)
    all_gather x5, waiting for transfers between devices, rows_gathered(): return lax.all_gather(piece, 'row', axis=0)  148 us
    ppermute x8, waiting for transfers between devices, shifted(): return lax.ppermute(x, axis, pairs)  86.4 us
    ppermute x4, waiting for transfers between devices, swapped(): return lax.ppermute(x, 'groups', [(i, count - 1 - i) for i in range(count)])  67.6 us
    ppermute x2, waiting for transfers between devices, on_device_sharing(): earlier.append(lax.ppermute(earlier[-1], ('col', 'sub'), up))  44.5 us
    dot_general x6, matrix products, add_panel(): return jnp.dot(normed, panel, preferred_element_type=jnp.float32)  40.2 us
    dot_general x4, local copies, waits for them, and re-layouts, add_panel(): return jnp.dot(normed, panel, preferred_element_type=jnp.float32)  22.9 us
    sub x2, matrix products, attend(): exponent = jnp.exp(scores - row_max)  21.7 us
    unnamed x38, local copies, waits for them, and re-layouts  18.1 us
  transfers between devices with their start and end apart: 22, of which 11 were waited for; matrix products, arithmetic and copies ran while one was open for 30% of the time, Pallas kernels for 0%

profile of v1, /device:TPU:22, one launch (start us, length us, event | category | flops | bytes accessed | tf_op | source)
XLA Modules:
  0.0 566.5 jit_solution(2977495785025421930)
XLA Ops:
  16.6 30.2 %collective-permute-done = bf16[512,1344]{0,1:T(8,128)(2,1)} collective-permute-done((bf16[512,1344]{0,1:T(8,128)(2,1)}, bf16[512,1344]{0,1:T(8,128)(2,1)}, u32[]{:S(2)}, u32[]{:S(2)}) %collective-permute-start) | collective-permute-done | bytes 1376288 | tf_op jit(solution)/shard_map/ppermute | solution.py:203
  50.5 14.3 %collective-permute-done.1 = bf16[512,1344]{0,1:T(8,128)(2,1)} collective-permute-done((bf16[512,1344]{0,1:T(8,128)(2,1)}, bf16[512,1344]{0,1:T(8,128)(2,1)}, u32[]{:S(2)}, u32[]{:S(2)}) %collective-permute-start.1) | collective-permute-done | bytes 1376288 | tf_op jit(solution)/shard_map/ppermute | solution.py:203
  74.1 48.8 %all-gather.19.cloned.1.call-done = bf16[5376,256]{1,0:T(8,128)(2,1)} async-done(((bf16[1344,256]{1,0:T(8,128)(2,1)}), bf16[5376,256]{1,0:T(8,128)(2,1)}) %all-gather.19.cloned.1.call-update) | async-done | bytes 2752528 | tf_op jit(solution)/shard_map/all_gather | solution.py:128
  125.9 99.2 %all-gather.21.cloned.1.call-done = bf16[5376,512]{1,0:T(8,128)(2,1)} async-done(((bf16[1344,512]{1,0:T(8,128)(2,1)}), bf16[5376,512]{1,0:T(8,128)(2,1)}) %all-gather.21.cloned.1.call-update) | async-done | bytes 5505040 | tf_op jit(solution)/shard_map/all_gather | solution.py:128
  240.0 5.8 %multiply_reduce_fusion.4 = (f32[512,2]{0,1:T(2,128)S(1)}, f32[512,2,128]{0,2,1:T(8,128)S(1)}) fusion(bf16[2,128,5376]{2,1,0:T(8,128)(2,1)} %bitcast.142, f32[5376]{0:T(1024)} %param.10, f32[512]{0:T(512)S(1)} %add_rsqrt_fusion.5, bf16[512,10752]{0,1:T(8,128)(2,1)} %constant_dynamic-update-slice_fusion, s32[]{:T(128)S(6)} %select_n.32), kind=kOutput, calls=%fused_computation.68 | convolution fusion | flops 1420557312 | bytes 8812548 | tf_op jit(solution)/shard_map/dot_general | solution.py:223
  245.8 7.1 %convolution_convert_fusion = bf16[512,256]{1,0:T(8,128)(2,1)} fusion(bf16[5376,256]{1,0:T(8,128)(2,1)} %bitcast.19, f32[5376]{0:T(1024)S(1)} %copy-done.12, f32[512]{0:T(512)S(1)} %add_rsqrt_fusion.5, bf16[512,10752]{0,1:T(8,128)(2,1)} %constant_dynamic-update-slice_fusion, s32[]{:T(128)S(6)} %select_n.32), kind=kOutput, calls=%fused_computation.45 | convolution fusion | flops 1420427264 | bytes 8543236 | tf_op jit(solution)/shard_map/dot_general | solution.py:223
  270.8 32.0 %collective-permute-done.9 = bf16[512,256]{1,0:T(8,128)(2,1)} collective-permute-done((bf16[512,256]{1,0:T(8,128)(2,1)}, bf16[512,256]{1,0:T(8,128)(2,1)}, u32[]{:S(2)}, u32[]{:S(2)}) %collective-permute-start.9) | collective-permute-done | bytes 262176 | tf_op jit(solution)/shard_map/ppermute | solution.py:15
  305.2 8.4 %copy.30 = bf16[512,5376]{1,0:T(8,128)(2,1)} copy(bf16[512,5376]{0,1:T(8,128)(2,1)} %bitcast.135) | data formatting | bytes 11010048 | tf_op jit(solution)/shard_map/dot_general | solution.py:223
  313.6 8.5 %multiply_reduce_fusion.2 = (f32[512,4]{0,1:T(4,128)S(1)}, f32[512,4,128]{0,2,1:T(8,128)}) fusion(bf16[4,128,5376]{2,1,0:T(8,128)(2,1)} %bitcast.137, f32[5376]{0:T(1024)S(1)} %copy-done.13, f32[512]{0:T(512)S(1)} %add_rsqrt_fusion.5, bf16[512,10752]{0,1:T(8,128)(2,1)} %constant_dynamic-update-slice_fusion, s32[]{:T(128)S(6)} %select_n.32), kind=kOutput, calls=%fused_computation.52 | convolution fusion | flops 2830104576 | bytes 12090372 | tf_op jit(solution)/shard_map/dot_general | solution.py:223
  322.1 23.6 %collective-permute-done.13 = bf16[4,1344,512]{2,1,0:T(8,128)(2,1)} collective-permute-done((bf16[4,1344,512]{2,1,0:T(8,128)(2,1)}, bf16[4,1344,512]{2,1,0:T(8,128)(2,1)}, u32[]{:S(2)}, u32[]{:S(2)}) %collective-permute-start.13) | collective-permute-done | bytes 5505056 | tf_op jit(solution)/shard_map/ppermute | solution.py:124
  345.7 8.3 %copy.39 = bf16[512,5376]{1,0:T(8,128)(2,1)} copy(bf16[512,5376]{0,1:T(8,128)(2,1)} %bitcast.35) | data formatting | bytes 11010048 | tf_op jit(solution)/shard_map/dot_general | solution.py:223
  354.0 7.5 %multiply_reduce_fusion.1 = (f32[512,4]{0,1:T(4,128)S(1)}, f32[512,4,128]{0,2,1:T(8,128)S(1)}) fusion(bf16[4,128,5376]{2,1,0:T(8,128)(2,1)} %bitcast.136, f32[5376]{0:T(1024)S(1)} %copy-done.13, f32[512]{0:T(512)S(1)} %add_rsqrt_fusion.5, bf16[512,10752]{0,1:T(8,128)(2,1)} %constant_dynamic-update-slice_fusion, s32[]{:T(128)S(6)} %select_n.32), kind=kOutput, calls=%fused_computation.50 | convolution fusion | flops 2830104576 | bytes 12090372 | tf_op jit(solution)/shard_map/dot_general | solution.py:223
  363.0 11.0 %fusion.55 = (f32[2,2,512]{2,1,0:T(2,128)S(1)}, f32[2,2,512,1536]{2,3,1,0:T(8,128)}) fusion(pred[512,1536]{0,1:T(8,128)(4,1)} %fusion.25, bf16[512,2,128]{0,2,1:T(8,128)(2,1)} %maximum_convert_fusion.1, bf16[512,2,128]{0,2,1:T(8,128)(2,1)} %bitcast.30, bf16[512,2,128]{0,2,1:T(8,128)(2,1)} %bitcast.29, bf16[512,2,2,64]{3,0,2,1:T(8,128)(2,1)S(1)} %copy.42, ...), kind=kOutput, calls=%fused_computation.109 | convolution fusion | flops 821298688 | bytes 14688256 | tf_op jit(solution)/shard_map/sub | solution.py:161
  374.0 6.4 %fusion.30 = bf16[2,128,2,512]{3,1,2,0:T(8,128)(2,1)} fusion(bf16[1536,2,128,1]{0,2,3,1:T(8,128)(2,1)S(1)} %bitcast.147, f32[2,2,512,1536]{2,3,1,0:T(8,128)} %get-tuple-element.32, f32[2,2,512]{2,1,0:T(2,128)S(1)} %get-tuple-element.31), kind=kOutput, calls=%fused_computation.43 | convolution fusion | flops 811859968 | bytes 13901824 | tf_op jit(solution)/shard_map/hgqs,shd->qhgd/dot_general | solution.py:163
  380.7 6.4 %convolution_convert_fusion.1 = bf16[512,256]{1,0:T(8,128)(2,1)S(1)} fusion(bf16[5376,256]{1,0:T(8,128)(2,1)} %all-gather.17.cloned.1.call-done, f32[5376]{0:T(1024)S(1)} %copy-done.14, f32[512]{0:T(512)S(1)} %add_rsqrt_fusion.5, bf16[512,10752]{0,1:T(8,128)(2,1)} %constant_dynamic-update-slice_fusion, s32[]{:T(128)S(6)} %select_n.32), kind=kOutput, calls=%fused_computation.46 | convolution fusion | flops 1420427264 | bytes 8543236 | tf_op jit(solution)/shard_map/dot_general | solution.py:223
  395.2 9.5 %collective-permute-done.3 = bf16[512,256]{1,0:T(8,128)(2,1)S(1)} collective-permute-done((bf16[512,256]{1,0:T(8,128)(2,1)S(1)}, bf16[512,256]{1,0:T(8,128)(2,1)S(1)}, u32[]{:S(2)}, u32[]{:S(2)}) %collective-permute-start.3) | collective-permute-done | bytes 262176 | tf_op jit(solution)/shard_map/ppermute | solution.py:15
  404.6 30.4 %collective-permute-done.4 = bf16[512,256]{1,0:T(8,128)(2,1)S(1)} collective-permute-done((bf16[512,256]{1,0:T(8,128)(2,1)S(1)}, bf16[512,256]{1,0:T(8,128)(2,1)S(1)}, u32[]{:S(2)}, u32[]{:S(2)}) %collective-permute-start.4) | collective-permute-done | bytes 262176 | tf_op jit(solution)/shard_map/ppermute | solution.py:15
  436.0 13.8 %collective-permute-done.6 = bf16[512,256]{0,1:T(8,128)(2,1)} collective-permute-done((bf16[512,256]{0,1:T(8,128)(2,1)}, bf16[512,256]{0,1:T(8,128)(2,1)}, u32[]{:S(2)}, u32[]{:S(2)}) %collective-permute-start.6) | collective-permute-done | bytes 262176 | tf_op jit(solution)/shard_map/ppermute | solution.py:15
  449.7 10.7 %fusion.56 = (f32[2,2,512]{2,1,0:T(2,128)S(1)}, f32[2,2,512,1536]{2,3,1,0:T(8,128)}) fusion(pred[512,1536]{0,1:T(8,128)(4,1)S(1)} %copy-done.5, bf16[512,2,128]{0,2,1:T(8,128)(2,1)} %maximum_convert_fusion, bf16[512,2,128]{0,2,1:T(8,128)(2,1)} %bitcast.8, bf16[512,2,128]{0,2,1:T(8,128)(2,1)} %bitcast.7, bf16[512,2,2,64]{3,0,2,1:T(8,128)(2,1)S(1)} %copy.33, ...), kind=kOutput, calls=%fused_computation.110 | convolution fusion | flops 821298688 | bytes 14688256 | tf_op jit(solution)/shard_map/sub | solution.py:161
  460.4 6.5 %fusion.31 = bf16[2,128,2,512]{3,1,2,0:T(8,128)(2,1)} fusion(bf16[1536,2,128,1]{0,2,3,1:T(8,128)(2,1)S(1)} %bitcast.148, f32[2,2,512,1536]{2,3,1,0:T(8,128)} %get-tuple-element.34, f32[2,2,512]{2,1,0:T(2,128)S(1)} %get-tuple-element.33), kind=kOutput, calls=%fused_computation.44 | convolution fusion | flops 811859968 | bytes 13901824 | tf_op jit(solution)/shard_map/hgqs,shd->qhgd/dot_general | solution.py:163
  466.9 8.6 %copy.50 = bf16[2048,1344]{1,0:T(8,128)(2,1)} copy(bf16[2048,1344]{0,1:T(8,128)(2,1)} %all-gather.23.cloned.1.call-done) | data formatting | bytes 11010048 | tf_op jit(solution)/shard_map/all_gather | solution.py:128
  493.1 7.3 %convolution_add_fusion = f32[512,1344]{0,1:T(8,128)S(1)} fusion(f32[512,1344]{0,1:T(8,128)} %convolution_bitcast_fusion.1, bf16[2048,1344]{0,1:T(8,128)(2,1)} %all-gather.23.cloned.1.call-done, bf16[512,2048]{0,1:T(8,128)(2,1)} %all-gather.13.cloned.1.call-done), kind=kOutput, calls=%fused_computation.33 | convolution fusion | flops 2819260416 | bytes 13107200 | tf_op jit(solution)/shard_map/dot_general | solution.py:243
  500.4 44.0 %collective-permute-done.14 = bf16[4,256,1344]{1,2,0:T(8,128)(2,1)} collective-permute-done((bf16[4,256,1344]{1,2,0:T(8,128)(2,1)S(1)}, bf16[4,256,1344]{1,2,0:T(8,128)(2,1)}, u32[]{:S(2)}, u32[]{:S(2)}) %collective-permute-start.14) | collective-permute-done | bytes 2752544 | tf_op jit(solution)/shard_map/ppermute | solution.py:124
  549.5 6.0 %psum.7 = f32[512]{0:T(512)S(1)} all-reduce(f32[512]{0:T(512)S(1)} %get-tuple-element.35), channel_id=1, replica_groups=mesh['groups'=2,'row'=4,'col'=2,'sub'=2] {'col','sub'}, use_global_device_ids=true, to_apply=%region_10.11 | all-reduce | flops 512 | bytes 4096 | tf_op jit(solution)/shard_map/psum | solution.py:257
  (119 shorter events, 98.0 us)
Async XLA Ops:
  6.5 63.3 %all-gather.17.cloned.1.call-start = ((), (), s32[]{:S(2)}) async-start(), calls=%async_computation.2 | async-start | bytes 3440640 | tf_op jit(solution)/shard_map/all_gather | solution.py:128
  8.7 114.1 %all-gather.19.cloned.1.call-start = ((), (), s32[]{:S(2)}) async-start(), calls=%async_computation.3 | async-start | bytes 3440640 | tf_op jit(solution)/shard_map/all_gather | solution.py:128
  10.8 214.3 %all-gather.21.cloned.1.call-start = ((), (), s32[]{:S(2)}) async-start(), calls=%async_computation.4 | async-start | bytes 6881280 | tf_op jit(solution)/shard_map/all_gather | solution.py:128
  13.4 453.5 %all-gather.23.cloned.1.call-start = ((), (), s32[]{:S(2)}) async-start(), calls=%async_computation.5 | async-start | bytes 6881280 | tf_op jit(solution)/shard_map/all_gather | solution.py:128
  14.7 468.5 %all-gather.25.cloned.1.call-start = ((), (), s32[]{:S(2)}) async-start(), calls=%async_computation.6 | async-start | bytes 3440640 | tf_op jit(solution)/shard_map/all_gather | solution.py:128
  14.8 32.0 %collective-permute-start = (bf16[512,1344]{0,1:T(8,128)(2,1)}, bf16[512,1344]{0,1:T(8,128)(2,1)}, u32[]{:S(2)}, u32[]{:S(2)}) collective-permute-start(bf16[512,1344]{0,1:T(8,128)(2,1)} %param.9), channel_id=1, source_target_pairs={{0,1},{1,2},{2,3},{3,0},{4,5},{5,6},{6,7},{7,4},{8,9},{9,10},{10,1... | collective-permute-start | bytes 4128776 | tf_op jit(solution)/shard_map/ppermute | solution.py:203
  14.8 56.7 %collective-permute-start.2 = (bf16[512,1344]{0,1:T(8,128)(2,1)}, bf16[512,1344]{0,1:T(8,128)(2,1)}, u32[]{:S(2)}, u32[]{:S(2)}) collective-permute-start(bf16[512,1344]{0,1:T(8,128)(2,1)} %param.9), channel_id=1, source_target_pairs={{0,3},{1,0},{2,1},{3,2},{4,7},{5,4},{6,5},{7,6},{8,11},{9,8},{10,9... | collective-permute-start | bytes 4128776 | tf_op jit(solution)/shard_map/ppermute | solution.py:205
  46.8 18.1 %collective-permute-start.1 = (bf16[512,1344]{0,1:T(8,128)(2,1)}, bf16[512,1344]{0,1:T(8,128)(2,1)}, u32[]{:S(2)}, u32[]{:S(2)}) collective-permute-start(bf16[512,1344]{0,1:T(8,128)(2,1)} %collective-permute-done), channel_id=1, source_target_pairs={{0,1},{1,2},{2,3},{3,0},{4,5},{5,6},{6,7},{7,4},{8,9},{9,10},{10,1... | collective-permute-start | bytes 4128776 | tf_op jit(solution)/shard_map/ppermute | solution.py:203
  47.8 439.9 %all-gather.15.cloned.1.call-start = ((), (), s32[]{:S(2)}) async-start(), calls=%async_computation.1 | async-start | bytes 2621440 | tf_op jit(solution)/shard_map/all_gather | solution.py:239
  69.9 175.9 %collective-permute-start.7 = (bf16[4,1344,256]{2,1,0:T(8,128)(2,1)}, bf16[4,1344,256]{2,1,0:T(8,128)(2,1)}, u32[]{:S(2)}, u32[]{:S(2)}) collective-permute-start(bf16[4,1344,256]{2,1,0:T(8,128)(2,1)} %bitcast.151), channel_id=1, source_target_pairs={{0,16},{16,0},{1,17},{17,1},{2,18},{18,2},{3,19},{19,3},{4,20},{20... | collective-permute-start | bytes 8257544 | tf_op jit(solution)/shard_map/ppermute | solution.py:124
  122.9 133.9 %collective-permute-start.10 = (bf16[4,1344,256]{2,1,0:T(8,128)(2,1)}, bf16[4,1344,256]{2,1,0:T(8,128)(2,1)}, u32[]{:S(2)}, u32[]{:S(2)}) collective-permute-start(bf16[4,1344,256]{2,1,0:T(8,128)(2,1)} %bitcast.139), channel_id=1, source_target_pairs={{0,16},{16,0},{1,17},{17,1},{2,18},{18,2},{3,19},{19,3},{4,20},{20... | collective-permute-start | bytes 8257544 | tf_op jit(solution)/shard_map/ppermute | solution.py:124
  225.1 120.6 %collective-permute-start.13 = (bf16[4,1344,512]{2,1,0:T(8,128)(2,1)}, bf16[4,1344,512]{2,1,0:T(8,128)(2,1)}, u32[]{:S(2)}, u32[]{:S(2)}) collective-permute-start(bf16[4,1344,512]{2,1,0:T(8,128)(2,1)} %bitcast.134), channel_id=1, source_target_pairs={{0,16},{16,0},{1,17},{17,1},{2,18},{18,2},{3,19},{19,3},{4,20},{20... | collective-permute-start | bytes 16515080 | tf_op jit(solution)/shard_map/ppermute | solution.py:124
  252.9 17.9 %collective-permute-start.8 = (bf16[512,256]{1,0:T(8,128)(2,1)}, bf16[512,256]{1,0:T(8,128)(2,1)}, u32[]{:S(2)}, u32[]{:S(2)}) collective-permute-start(bf16[512,256]{1,0:T(8,128)(2,1)} %convolution_convert_fusion), channel_id=1, source_target_pairs={{0,8},{4,12},{1,9},{5,13},{2,10},{6,14},{3,11},{7,15},{16,24},{20,... | collective-permute-start | bytes 786440 | tf_op jit(solution)/shard_map/ppermute | solution.py:15
  254.2 48.7 %collective-permute-start.9 = (bf16[512,256]{1,0:T(8,128)(2,1)}, bf16[512,256]{1,0:T(8,128)(2,1)}, u32[]{:S(2)}, u32[]{:S(2)}) collective-permute-start(bf16[512,256]{1,0:T(8,128)(2,1)} %convolution_convert_fusion), channel_id=1, source_target_pairs={{0,4},{4,8},{8,12},{1,5},{5,9},{9,13},{2,6},{6,10},{10,14},{3,7},{... | collective-permute-start | bytes 786440 | tf_op jit(solution)/shard_map/ppermute | solution.py:15
  266.8 96.1 %collective-permute-start.11 = (bf16[512,256]{0,1:T(8,128)(2,1)}, bf16[512,256]{0,1:T(8,128)(2,1)}, u32[]{:S(2)}, u32[]{:S(2)}) collective-permute-start(bf16[512,256]{0,1:T(8,128)(2,1)} %bitcast.28), channel_id=1, source_target_pairs={{0,8},{4,12},{1,9},{5,13},{2,10},{6,14},{3,11},{7,15},{16,24},{20,... | collective-permute-start | bytes 786440 | tf_op jit(solution)/shard_map/ppermute | solution.py:15
  268.1 94.9 %collective-permute-start.12 = (bf16[512,256]{0,1:T(8,128)(2,1)}, bf16[512,256]{0,1:T(8,128)(2,1)}, u32[]{:S(2)}, u32[]{:S(2)}) collective-permute-start(bf16[512,256]{0,1:T(8,128)(2,1)} %bitcast.28), channel_id=1, source_target_pairs={{0,4},{4,8},{8,12},{1,5},{5,9},{9,13},{2,6},{6,10},{10,14},{3,7},{... | collective-permute-start | bytes 786440 | tf_op jit(solution)/shard_map/ppermute | solution.py:15
  380.4 69.3 %copy-start.5 = (pred[512,1536]{0,1:T(8,128)(4,1)S(1)}, pred[512,1536]{0,1:T(8,128)(4,1)}, u32[]{:S(2)}) copy-start(pred[512,1536]{0,1:T(8,128)(4,1)} %fusion.25) | copy-start | bytes 2359300
  380.4 112.7 %all-gather.13.cloned.1.call-start = ((), (), s32[]{:S(2)}) async-start(), calls=%async_computation | async-start | bytes 2621440 | tf_op jit(solution)/shard_map/all_gather | solution.py:239
  387.1 17.6 %collective-permute-start.3 = (bf16[512,256]{1,0:T(8,128)(2,1)S(1)}, bf16[512,256]{1,0:T(8,128)(2,1)S(1)}, u32[]{:S(2)}, u32[]{:S(2)}) collective-permute-start(bf16[512,256]{1,0:T(8,128)(2,1)S(1)} %convolution_convert_fusion.1), channel_id=1, source_target_pairs={{0,8},{4,12},{1,9},{5,13},{2,10},{6,14},{3,11},{7,15},{16,24},{20,... | collective-permute-start | bytes 786440 | tf_op jit(solution)/shard_map/ppermute | solution.py:15
  388.4 46.7 %collective-permute-start.4 = (bf16[512,256]{1,0:T(8,128)(2,1)S(1)}, bf16[512,256]{1,0:T(8,128)(2,1)S(1)}, u32[]{:S(2)}, u32[]{:S(2)}) collective-permute-start(bf16[512,256]{1,0:T(8,128)(2,1)S(1)} %convolution_convert_fusion.1), channel_id=1, source_target_pairs={{0,4},{4,8},{8,12},{1,5},{5,9},{9,13},{2,6},{6,10},{10,14},{3,7},{... | collective-permute-start | bytes 786440 | tf_op jit(solution)/shard_map/ppermute | solution.py:15
  392.0 44.0 %collective-permute-start.5 = (bf16[512,256]{0,1:T(8,128)(2,1)}, bf16[512,256]{0,1:T(8,128)(2,1)}, u32[]{:S(2)}, u32[]{:S(2)}) collective-permute-start(bf16[512,256]{0,1:T(8,128)(2,1)} %bitcast.6), channel_id=1, source_target_pairs={{0,8},{4,12},{1,9},{5,13},{2,10},{6,14},{3,11},{7,15},{16,24},{20,... | collective-permute-start | bytes 786440 | tf_op jit(solution)/shard_map/ppermute | solution.py:15
  393.2 56.5 %collective-permute-start.6 = (bf16[512,256]{0,1:T(8,128)(2,1)}, bf16[512,256]{0,1:T(8,128)(2,1)}, u32[]{:S(2)}, u32[]{:S(2)}) collective-permute-start(bf16[512,256]{0,1:T(8,128)(2,1)} %bitcast.6), channel_id=1, source_target_pairs={{0,4},{4,8},{8,12},{1,5},{5,9},{9,13},{2,6},{6,10},{10,14},{3,7},{... | collective-permute-start | bytes 786440 | tf_op jit(solution)/shard_map/ppermute | solution.py:15
  482.6 61.8 %collective-permute-start.14 = (bf16[4,256,1344]{1,2,0:T(8,128)(2,1)S(1)}, bf16[4,256,1344]{1,2,0:T(8,128)(2,1)}, u32[]{:S(2)}, u32[]{:S(2)}) collective-permute-start(bf16[4,256,1344]{1,2,0:T(8,128)(2,1)S(1)} %copy.75), channel_id=1, source_target_pairs={{0,16},{16,0},{1,17},{17,1},{2,18},{18,2},{3,19},{19,3},{4,20},{20... | collective-permute-start | bytes 8257544 | tf_op jit(solution)/shard_map/ppermute | solution.py:124
  500.4 55.1 %copy-start.8 = (f32[1344]{0:T(1024)S(1)}, f32[1344]{0:T(1024)}, u32[]{:S(2)}) copy-start(f32[1344]{0:T(1024)} %param.17) | copy-start | bytes 16132
  (13 other events, 166.1 us)
Sparse Core Ops, SparseCore 0:
  8.9 56.6 all-gather.16
  67.2 55.6 all-gather.18
  124.4 100.6 all-gather.20
  226.5 118.9 all-gather.22
  347.0 89.8 all-gather.24
  438.3 27.7 all-gather.14
  467.6 22.4 all-gather.12
